TPU v7x, 32 devices: a whole 2x2x4 slice. The times are simulated.
32 devices in a mesh: tm: 8 (over z, x), strip: 4 (over y, core).
Axes of the slice: x: 2, y: 2, z: 4, core: 2. Of those that a mesh axis runs over, the one named last changes fastest.
Arguments:
- coarse_feat: bfloat16 [32, 48, 4, 384], P('tm', 'strip'), may hold values from -6 to 6
- coarse_gain: float32 [384], replicated, may hold values from 0.5 to 2
- coarse_weight: bfloat16 [3, 3, 3, 384, 384], replicated, may hold values from -0.0625 to 0.0625
- coarse_bias: float32 [384], replicated, may hold values from -3 to 3
- up_weight: bfloat16 [3, 3, 384, 192], replicated, may hold values from -0.109375 to 0.109375
- up_bias: float32 [192], replicated, may hold values from -3 to 3
- fine_gain: float32 [192], replicated, may hold values from 0.5 to 2
- fine_weight: bfloat16 [3, 3, 3, 192, 192], replicated, may hold values from -0.078125 to 0.078125
- fine_bias: float32 [192], replicated, may hold values from -3 to 3
Outputs:
- decoded: bfloat16 [32, 96, 8, 192], P('tm', 'strip')
All inputs are finite; a program needn't handle non-finite values.
Results may differ from a plain program's by a relative error of at most 0.0095.
Values may be sent and summed in bfloat16 or wider, within the bound.
A program may use at most 64 MiB of HBM per device.

v0:
```python
import jax
import jax.numpy as jnp
from jax import lax
from jax.sharding import PartitionSpec as P

eps = 1e-06


def passed_along(value, axis, steps):
    count = lax.axis_size(axis)
    first, last = (max(0, -steps), min(count, count - steps))
    return lax.ppermute(value, axis, [(source, source + steps) for source in range(first, last)])


def extended_2(block, sides, width):
    for axis, dim in sides:
        count = lax.axis_size(axis)
        forward = [(i, i + 1) for i in range(count - 1)]
        backward = [(target, source) for source, target in forward]
        low = lax.ppermute(
            lax.slice_in_dim(block, block.shape[dim] - width, None, axis=dim), axis, forward
        )
        high = lax.ppermute(lax.slice_in_dim(block, 0, width, axis=dim), axis, backward)
        block = jnp.concatenate([low, block, high], axis=dim)
    return block


def prep(feat, gain):
    values = feat.astype(jnp.float32)
    meansq = jnp.mean(values * values, axis=-1, keepdims=True)
    return jax.nn.silu(values * lax.rsqrt(meansq + eps) * gain).astype(jnp.bfloat16)


def conv_cube(act, kernel, rows_out):
    frames_out = act.shape[0] - 2
    width = act.shape[2]
    padded = jnp.pad(act, ((0, 0), (0, 0), (1, 1), (0, 0)))
    total = jnp.zeros((frames_out * rows_out * width, kernel.shape[4]), jnp.float32)
    for tstep in range(3):
        for rstep in range(3):
            for cstep in range(3):
                piece = padded[
                    tstep : tstep + frames_out, rstep : rstep + rows_out, cstep : cstep + width
                ]
                total = total + jnp.dot(
                    piece.reshape(-1, piece.shape[3]),
                    kernel[tstep, rstep, cstep],
                    preferred_element_type=jnp.float32,
                )
    return total.reshape(frames_out, rows_out, width, kernel.shape[4])


def conv_plane(act, kernel, rows_out):
    frames = act.shape[0]
    width = act.shape[2]
    padded = jnp.pad(act, ((0, 0), (0, 0), (1, 1), (0, 0)))
    total = jnp.zeros((frames * rows_out * width, kernel.shape[3]), jnp.float32)
    for rstep in range(3):
        for cstep in range(3):
            piece = padded[:, rstep : rstep + rows_out, cstep : cstep + width]
            total = total + jnp.dot(
                piece.reshape(-1, piece.shape[3]),
                kernel[rstep, cstep],
                preferred_element_type=jnp.float32,
            )
    return total.reshape(frames, rows_out, width, kernel.shape[3])


def row_keep(count, first, limit):
    rows = first + jnp.arange(count, dtype=jnp.int32)
    return ((rows >= 0) & (rows < limit))[None, :, None, None]


def local(
    coarse_feat,
    coarse_gain,
    coarse_weight,
    coarse_bias,
    up_weight,
    up_bias,
    fine_gain,
    fine_weight,
    fine_bias,
):
    frames, strip_rows = (coarse_feat.shape[0], coarse_feat.shape[1])
    strips = lax.axis_size("strip")
    place = lax.axis_index("strip")
    past = passed_along(coarse_feat[frames - 2 :], "tm", 1)
    extended = jnp.concatenate([past, coarse_feat], axis=0)
    margined = extended_2(extended, (("strip", 1),), 2)
    act0 = prep(margined, coarse_gain)
    coarse = conv_cube(act0, coarse_weight, strip_rows + 2) + coarse_bias
    coarse = jnp.where(
        row_keep(strip_rows + 2, place * strip_rows - 1, strips * strip_rows), coarse, 0.0
    ).astype(jnp.bfloat16)
    upper = jnp.repeat(jnp.repeat(coarse, 2, axis=1), 2, axis=2)
    lifted = conv_plane(upper, up_weight, 2 * strip_rows + 2) + up_bias
    lifted = jnp.where(
        row_keep(2 * strip_rows + 2, 2 * place * strip_rows - 1, 2 * strips * strip_rows),
        lifted,
        0.0,
    )
    lifted_own = lifted.astype(jnp.bfloat16)
    cached = passed_along(lifted_own[frames - 2 :], "tm", 1)
    lifted_all = jnp.concatenate([cached, lifted_own], axis=0)
    act1 = prep(lifted_all, fine_gain)
    fine = conv_cube(act1, fine_weight, 2 * strip_rows) + fine_bias
    residual = lifted_all[2:, 1 : 2 * strip_rows + 1].astype(jnp.float32)
    return (fine + residual).astype(jnp.bfloat16)


def solution(mesh):
    placed = (P("tm", "strip", None, None), P(), P(), P(), P(), P(), P(), P(), P())
    return jax.shard_map(
        local, mesh=mesh, in_specs=placed, out_specs=P("tm", "strip", None, None), check_vma=False
    )
```

profile of v0, /device:TPU:9, one launch (start us, length us, event | category | flops | bytes accessed | tf_op | source)
XLA Modules:
  0.0 83.4 jit_solution(4426951985623130338)
XLA Ops:
  0.9 3.1 %collective-permute-start = (bf16[2,12,4,384]{3,2,1,0:T(4,128)(2,1)S(1)}, bf16[2,12,4,384]{3,2,1,0:T(4,128)(2,1)S(1)}, u32[]{:S(2)}, u32[]{:S(2)}) collective-permute-start(bf16[2,12,4,384]{3,2,1,0:T(4,128)(2,1)S(1)} %slice.414), channel_id=1, source_target_pairs={{0,4},{4,8},{8,12},{12,16},{16,20},{20,24},{24,28},{1,5},{5,9},{9,... | collective-permute-start | bytes 221192 | tf_op jit(solution)/shard_map/ppermute | solution.py:12
  4.1 2.8 %collective-permute-done = bf16[2,12,4,384]{3,2,1,0:T(4,128)(2,1)S(1)} collective-permute-done((bf16[2,12,4,384]{3,2,1,0:T(4,128)(2,1)S(1)}, bf16[2,12,4,384]{3,2,1,0:T(4,128)(2,1)S(1)}, u32[]{:S(2)}, u32[]{:S(2)}) %collective-permute-start) | collective-permute-done | bytes 73760 | tf_op jit(solution)/shard_map/ppermute | solution.py:12
  8.0 4.9 %collective-permute-start.1 = (bf16[6,2,4,384]{3,2,1,0:T(4,128)(2,1)S(1)}, bf16[6,2,4,384]{3,2,1,0:T(4,128)(2,1)S(1)}, u32[]{:S(2)}, u32[]{:S(2)}) collective-permute-start(bf16[6,2,4,384]{3,2,1,0:T(4,128)(2,1)S(1)} %get-tuple-element.68), channel_id=1, source_target_pairs={{0,1},{1,2},{2,3},{4,5},{5,6},{6,7},{8,9},{9,10},{10,11},{12,13},{... | collective-permute-start | bytes 110600 | tf_op jit(solution)/shard_map/ppermute | solution.py:20
  12.8 1.9 %collective-permute-start.2 = (bf16[6,2,4,384]{3,2,1,0:T(4,128)(2,1)S(1)}, bf16[6,2,4,384]{3,2,1,0:T(4,128)(2,1)S(1)}, u32[]{:S(2)}, u32[]{:S(2)}) collective-permute-start(bf16[6,2,4,384]{3,2,1,0:T(4,128)(2,1)S(1)} %get-tuple-element.69), channel_id=1, source_target_pairs={{1,0},{2,1},{3,2},{5,4},{6,5},{7,6},{9,8},{10,9},{11,10},{13,12},{... | collective-permute-start | bytes 110600 | tf_op jit(solution)/shard_map/ppermute | solution.py:23
  14.8 3.3 %collective-permute-done.2 = bf16[6,2,4,384]{3,2,1,0:T(4,128)(2,1)S(1)} collective-permute-done((bf16[6,2,4,384]{3,2,1,0:T(4,128)(2,1)S(1)}, bf16[6,2,4,384]{3,2,1,0:T(4,128)(2,1)S(1)}, u32[]{:S(2)}, u32[]{:S(2)}) %collective-permute-start.2) | collective-permute-done | bytes 36896 | tf_op jit(solution)/shard_map/ppermute | solution.py:23
  19.9 2.6 %pad_slice_fusion.24 = (bf16[4,14,4,384]{3,2,1,0:T(4,128)(2,1)}, bf16[4,14,4,384]{3,2,1,0:T(4,128)(2,1)}, bf16[4,14,4,384]{3,2,1,0:T(4,128)(2,1)}, bf16[4,14,4,3...) fusion(bf16[6,16,4,384]{3,2,1,0:T(4,128)(2,1)S(1)} %fusion.13), kind=kLoop, calls=%fused_computation.24 | loop fusion | bytes 3907584 | tf_op jit(solution)/shard_map/slice | solution.py:42
  25.2 1.6 %reshape.241 = bf16[224,384]{1,0:T(8,128)(2,1)} reshape(bf16[4,14,4,384]{3,2,1,0:T(4,128)(2,1)} %get-tuple-element.42) | data formatting | bytes 344064 | tf_op jit(solution)/shard_map/reshape | solution.py:46
  26.8 1.6 %reshape.242 = bf16[224,384]{1,0:T(8,128)(2,1)} reshape(bf16[4,14,4,384]{3,2,1,0:T(4,128)(2,1)} %get-tuple-element.43) | data formatting | bytes 344064 | tf_op jit(solution)/shard_map/reshape | solution.py:46
  28.5 1.6 %reshape.244 = bf16[224,384]{1,0:T(8,128)(2,1)} reshape(bf16[4,14,4,384]{3,2,1,0:T(4,128)(2,1)} %get-tuple-element.44) | data formatting | bytes 344064 | tf_op jit(solution)/shard_map/reshape | solution.py:46
  30.1 1.6 %reshape.245 = bf16[224,384]{1,0:T(8,128)(2,1)} reshape(bf16[4,14,4,384]{3,2,1,0:T(4,128)(2,1)} %get-tuple-element.45) | data formatting | bytes 344064 | tf_op jit(solution)/shard_map/reshape | solution.py:46
  31.7 1.6 %reshape.247 = bf16[224,384]{1,0:T(8,128)(2,1)} reshape(bf16[4,14,4,384]{3,2,1,0:T(4,128)(2,1)} %get-tuple-element.46) | data formatting | bytes 344064 | tf_op jit(solution)/shard_map/reshape | solution.py:46
  35.9 1.4 %fusion.40 = f32[224,384]{1,0:T(8,128)S(1)} fusion(bf16[224,384]{1,0:T(8,128)(2,1)} %reshape.239, bf16[3,3,3,384,384]{4,3,2,1,0:T(8,128)(2,1)} %param.11), kind=kOutput, calls=%fused_computation.152 | convolution fusion | flops 66060288 | bytes 811008 | tf_op jit(solution)/shard_map/dot_general | solution.py:45
  37.3 1.4 %convolution_add_fusion.59 = f32[224,384]{1,0:T(8,128)S(1)} fusion(f32[224,384]{1,0:T(8,128)S(1)} %fusion.40, bf16[224,384]{1,0:T(8,128)(2,1)} %reshape.240, bf16[3,3,3,384,384]{4,3,2,1,0:T(8,128)(2,1)} %param.11), kind=kOutput, calls=%fused_computation.111 | convolution fusion | flops 66146304 | bytes 1155072 | tf_op jit(solution)/shard_map/dot_general | solution.py:45
  38.7 1.3 %convolution_add_fusion.58 = f32[224,384]{1,0:T(8,128)S(1)} fusion(f32[224,384]{1,0:T(8,128)S(1)} %convolution_add_fusion.59, bf16[224,384]{1,0:T(8,128)(2,1)} %reshape.241, bf16[3,3,3,384,384]{4,3,2,1,0:T(8,128)(2,1)} %param.11), kind=kOutput, calls=%fused_computation.110 | convolution fusion | flops 66146304 | bytes 1155072 | tf_op jit(solution)/shard_map/dot_general | solution.py:45
  40.0 1.3 %convolution_add_fusion.57 = f32[224,384]{1,0:T(8,128)S(1)} fusion(f32[224,384]{1,0:T(8,128)S(1)} %convolution_add_fusion.58, bf16[224,384]{1,0:T(8,128)(2,1)} %reshape.242, bf16[3,3,3,384,384]{4,3,2,1,0:T(8,128)(2,1)} %param.11), kind=kOutput, calls=%fused_computation.109 | convolution fusion | flops 66146304 | bytes 1155072 | tf_op jit(solution)/shard_map/dot_general | solution.py:45
  42.6 1.2 %convolution_add_fusion.55 = f32[224,384]{1,0:T(8,128)S(1)} fusion(f32[224,384]{1,0:T(8,128)S(1)} %convolution_add_fusion.56, bf16[224,384]{1,0:T(8,128)(2,1)S(1)} %copy-done.4, bf16[3,3,3,384,384]{4,3,2,1,0:T(8,128)(2,1)} %param.11), kind=kOutput, calls=%fused_computation.107 | convolution fusion | flops 66146304 | bytes 1155072 | tf_op jit(solution)/shard_map/dot_general | solution.py:45
  43.9 1.4 %convolution_add_fusion.54 = f32[224,384]{1,0:T(8,128)S(1)} fusion(f32[224,384]{1,0:T(8,128)S(1)} %convolution_add_fusion.55, bf16[224,384]{1,0:T(8,128)(2,1)S(1)} %copy-done.3, bf16[3,3,3,384,384]{4,3,2,1,0:T(8,128)(2,1)} %param.11), kind=kOutput, calls=%fused_computation.106 | convolution fusion | flops 66146304 | bytes 1155072 | tf_op jit(solution)/shard_map/dot_general | solution.py:45
  45.2 1.2 %convolution_add_fusion.53 = f32[224,384]{1,0:T(8,128)S(1)} fusion(f32[224,384]{1,0:T(8,128)S(1)} %convolution_add_fusion.54, bf16[224,384]{1,0:T(8,128)(2,1)S(1)} %reshape.246, bf16[3,3,3,384,384]{4,3,2,1,0:T(8,128)(2,1)} %param.11), kind=kOutput, calls=%fused_computation.105 | convolution fusion | flops 66146304 | bytes 1155072 | tf_op jit(solution)/shard_map/dot_general | solution.py:45
  46.5 1.2 %convolution_add_fusion.52 = f32[224,384]{1,0:T(8,128)S(1)} fusion(f32[224,384]{1,0:T(8,128)S(1)} %convolution_add_fusion.53, bf16[224,384]{1,0:T(8,128)(2,1)S(1)} %copy-done.2, bf16[3,3,3,384,384]{4,3,2,1,0:T(8,128)(2,1)} %param.11), kind=kOutput, calls=%fused_computation.104 | convolution fusion | flops 66146304 | bytes 1155072 | tf_op jit(solution)/shard_map/dot_general | solution.py:45
  48.9 1.2 %convolution_add_fusion.50 = f32[224,384]{1,0:T(8,128)S(1)} fusion(f32[224,384]{1,0:T(8,128)S(1)} %convolution_add_fusion.51, bf16[224,384]{1,0:T(8,128)(2,1)S(1)} %reshape.249, bf16[3,3,3,384,384]{4,3,2,1,0:T(8,128)(2,1)} %param.11), kind=kOutput, calls=%fused_computation.102 | convolution fusion | flops 66146304 | bytes 1155072 | tf_op jit(solution)/shard_map/dot_general | solution.py:45
  50.1 1.2 %convolution_add_fusion.49 = f32[224,384]{1,0:T(8,128)S(1)} fusion(f32[224,384]{1,0:T(8,128)S(1)} %convolution_add_fusion.50, bf16[224,384]{1,0:T(8,128)(2,1)S(1)} %reshape.250, bf16[3,3,3,384,384]{4,3,2,1,0:T(8,128)(2,1)} %param.11), kind=kOutput, calls=%fused_computation.101 | convolution fusion | flops 66146304 | bytes 1155072 | tf_op jit(solution)/shard_map/dot_general | solution.py:45
  62.9 2.4 %collective-permute-start.3 = (bf16[2,26,8,192]{3,2,1,0:T(8,128)(2,1)S(1)}, bf16[2,26,8,192]{3,2,1,0:T(8,128)(2,1)S(1)}, u32[]{:S(2)}, u32[]{:S(2)}) collective-permute-start(bf16[2,26,8,192]{3,2,1,0:T(8,128)(2,1)S(1)} %slice.559), channel_id=1, source_target_pairs={{0,4},{4,8},{8,12},{12,16},{16,20},{20,24},{24,28},{1,5},{5,9},{9,... | collective-permute-start | bytes 479240 | tf_op jit(solution)/shard_map/ppermute | solution.py:12
  65.3 5.7 %collective-permute-done.3 = bf16[2,26,8,192]{3,2,1,0:T(8,128)(2,1)S(1)} collective-permute-done((bf16[2,26,8,192]{3,2,1,0:T(8,128)(2,1)S(1)}, bf16[2,26,8,192]{3,2,1,0:T(8,128)(2,1)S(1)}, u32[]{:S(2)}, u32[]{:S(2)}) %collective-permute-start.3) | collective-permute-done | bytes 159776 | tf_op jit(solution)/shard_map/ppermute | solution.py:12
  72.0 2.0 %pad_slice_fusion = (bf16[4,24,8,192]{3,2,1,0:T(8,128)(2,1)S(1)}, bf16[4,24,8,192]{3,2,1,0:T(8,128)(2,1)S(1)}, bf16[4,24,8,192]{3,2,1,0:T(8,128)(2,1)S(1)}, bf16...) fusion(bf16[6,26,8,192]{3,2,1,0:T(8,128)(2,1)S(1)} %fusion.7), kind=kLoop, calls=%fused_computation | loop fusion | bytes 7028736 | tf_op jit(solution)/shard_map/slice | solution.py:42
  (124 shorter events, 32.8 us)
Async XLA Ops:
  0.9 6.0 %collective-permute-start = (bf16[2,12,4,384]{3,2,1,0:T(4,128)(2,1)S(1)}, bf16[2,12,4,384]{3,2,1,0:T(4,128)(2,1)S(1)}, u32[]{:S(2)}, u32[]{:S(2)}) collective-permute-start(bf16[2,12,4,384]{3,2,1,0:T(4,128)(2,1)S(1)} %slice.414), channel_id=1, source_target_pairs={{0,4},{4,8},{8,12},{12,16},{16,20},{20,24},{24,28},{1,5},{5,9},{9,... | collective-permute-start | bytes 221192 | tf_op jit(solution)/shard_map/ppermute | solution.py:12
  8.0 6.8 %collective-permute-start.1 = (bf16[6,2,4,384]{3,2,1,0:T(4,128)(2,1)S(1)}, bf16[6,2,4,384]{3,2,1,0:T(4,128)(2,1)S(1)}, u32[]{:S(2)}, u32[]{:S(2)}) collective-permute-start(bf16[6,2,4,384]{3,2,1,0:T(4,128)(2,1)S(1)} %get-tuple-element.68), channel_id=1, source_target_pairs={{0,1},{1,2},{2,3},{4,5},{5,6},{6,7},{8,9},{9,10},{10,11},{12,13},{... | collective-permute-start | bytes 110600 | tf_op jit(solution)/shard_map/ppermute | solution.py:20
  12.8 5.3 %collective-permute-start.2 = (bf16[6,2,4,384]{3,2,1,0:T(4,128)(2,1)S(1)}, bf16[6,2,4,384]{3,2,1,0:T(4,128)(2,1)S(1)}, u32[]{:S(2)}, u32[]{:S(2)}) collective-permute-start(bf16[6,2,4,384]{3,2,1,0:T(4,128)(2,1)S(1)} %get-tuple-element.69), channel_id=1, source_target_pairs={{1,0},{2,1},{3,2},{5,4},{6,5},{7,6},{9,8},{10,9},{11,10},{13,12},{... | collective-permute-start | bytes 110600 | tf_op jit(solution)/shard_map/ppermute | solution.py:23
  35.8 6.7 %copy-start.4 = (bf16[224,384]{1,0:T(8,128)(2,1)S(1)}, bf16[224,384]{1,0:T(8,128)(2,1)}, u32[]{:S(2)}) copy-start(bf16[224,384]{1,0:T(8,128)(2,1)} %reshape.244) | copy-start | bytes 516100
  35.9 16.7 %slice-start = ((s8[7962624]{0:T(1024)(128)(4,1)}), s8[4194304]{0:T(1024)(128)(4,1)S(1)}, s32[]{:S(2)}) async-start(s8[7962624]{0:T(1024)(128)(4,1)} %bitcast.291), calls=%async_computation | async-start | bytes 8388608
  37.3 6.5 %copy-start.3 = (bf16[224,384]{1,0:T(8,128)(2,1)S(1)}, bf16[224,384]{1,0:T(8,128)(2,1)}, u32[]{:S(2)}) copy-start(bf16[224,384]{1,0:T(8,128)(2,1)} %reshape.245) | copy-start | bytes 516100
  40.0 6.4 %copy-start.2 = (bf16[224,384]{1,0:T(8,128)(2,1)S(1)}, bf16[224,384]{1,0:T(8,128)(2,1)}, u32[]{:S(2)}) copy-start(bf16[224,384]{1,0:T(8,128)(2,1)} %reshape.247) | copy-start | bytes 516100
  43.8 8.8 %slice-start.1 = ((s8[7962624]{0:T(1024)(128)(4,1)}), s8[3768320]{0:T(1024)(128)(4,1)S(1)}, s32[]{:S(2)}) async-start(s8[7962624]{0:T(1024)(128)(4,1)} %bitcast.291), calls=%async_computation.1 | async-start | bytes 7536640
  55.3 1.2 %copy-start.5 = (f32[384]{0:T(512)S(1)}, f32[384]{0:T(512)}, u32[]{:S(2)}) copy-start(f32[384]{0:T(512)} %param.12) | copy-start | bytes 4612
  57.4 1.3 %copy-start.1 = (bf16[3,3,384,192]{2,3,1,0:T(8,128)(2,1)S(1)}, bf16[3,3,384,192]{2,3,1,0:T(8,128)(2,1)}, u32[]{:S(2)}) copy-start(bf16[3,3,384,192]{2,3,1,0:T(8,128)(2,1)} %param.13) | copy-start | bytes 3981316
  61.6 1.1 %copy-start.7 = (f32[192]{0:T(256)S(1)}, f32[192]{0:T(256)}, u32[]{:S(2)}) copy-start(f32[192]{0:T(256)} %param.14) | copy-start | bytes 2308
  62.0 9.2 %copy-start.6 = (f32[192]{0:T(256)S(1)}, f32[192]{0:T(256)}, u32[]{:S(2)}) copy-start(f32[192]{0:T(256)} %param.15) | copy-start | bytes 2308
  62.9 8.1 %collective-permute-start.3 = (bf16[2,26,8,192]{3,2,1,0:T(8,128)(2,1)S(1)}, bf16[2,26,8,192]{3,2,1,0:T(8,128)(2,1)S(1)}, u32[]{:S(2)}, u32[]{:S(2)}) collective-permute-start(bf16[2,26,8,192]{3,2,1,0:T(8,128)(2,1)S(1)} %slice.559), channel_id=1, source_target_pairs={{0,4},{4,8},{8,12},{12,16},{16,20},{20,24},{24,28},{1,5},{5,9},{9,... | collective-permute-start | bytes 479240 | tf_op jit(solution)/shard_map/ppermute | solution.py:12
  72.0 2.0 %copy-start = (bf16[3,3,3,192,192]{4,3,2,1,0:T(8,128)(2,1)S(1)}, bf16[3,3,3,192,192]{4,3,2,1,0:T(8,128)(2,1)}, u32[]{:S(2)}) copy-start(bf16[3,3,3,192,192]{4,3,2,1,0:T(8,128)(2,1)} %param.16) | copy-start | bytes 5971972
  81.6 0.9 %copy-start.8 = (f32[192]{0:T(256)S(1)}, f32[192]{0:T(256)}, u32[]{:S(2)}) copy-start(f32[192]{0:T(256)} %param.17) | copy-start | bytes 2308
where the time goes:
time: 84.2 us; the launch traced here: 83.4 us
  matrix products  32 us (38%)
  local copies, waits for them, and re-layouts  23.2 us (28%)
  starting transfers between devices  12.3 us (15%)
  waiting for transfers between devices  11.8 us (14%)
  other arithmetic  3.24 us (4%)
    dot_general x54, matrix products, conv_cube(): jnp.dot(piece.reshape(-1, piece.shape[3]), kernel[tstep, rstep, cstep], p...  28.4 us
    reshape x27, local copies, waits for them, and re-layouts, conv_cube(): piece.reshape(-1, piece.shape[3])  13.3 us
    ppermute x2, waiting for transfers between devices, passed_along(): lax.ppermute(value, axis, [(source, source + steps) for source in range(f...  8.52 us
    ppermute x2, starting transfers between devices, passed_along(): lax.ppermute(value, axis, [(source, source + steps) for source in range(f...  5.52 us
    slice x4, local copies, waits for them, and re-layouts, conv_cube(): padded[tstep:tstep + frames_out, rstep:rstep + rows_out, cstep:cstep + wi...  5.16 us
    ppermute x1, starting transfers between devices, extended_2(): lax.ppermute(lax.slice_in_dim(block, block.shape[dim] - width, None, axis...  4.86 us
    dot_general x9, matrix products, conv_plane(): jnp.dot(piece.reshape(-1, piece.shape[3]), kernel[rstep, cstep], preferre...  3.57 us
    ppermute x1, waiting for transfers between devices, extended_2(): lax.ppermute(lax.slice_in_dim(block, 0, width, axis=dim), axis, backward)  3.32 us
  transfers between devices with their start and end apart: 4, of which 3 were waited for; matrix products, arithmetic and copies ran while one was open for 0% of the time, Pallas kernels for 0%

commit v1 on v0

v1 whole, which is shorter than its diff:
```python
import functools

import jax
import jax.numpy as jnp
from jax import lax
from jax.experimental import pallas as pl
from jax.experimental.pallas import tpu as pltpu
from jax.sharding import PartitionSpec as P

eps = 1e-06
F32, BF = jnp.float32, jnp.bfloat16


def prep(values, gain):
    meansq = jnp.mean(values * values, axis=-1, keepdims=True)
    v = values * lax.rsqrt(meansq + eps) * gain
    return (v / (1.0 + jnp.exp(-v))).astype(BF)


def body(dims, x_ref, g0_ref, wc_hbm, b0_ref, wu_hbm, bu_ref, g1_ref, wf_hbm, b1_ref, out_ref,
         wc, wu, wf, acts, acc, prod, fine, resid, facc, sems):
    frames, rows, cols, pad_rows, strips = dims
    c0, c1 = wc.shape[-1], wu.shape[-1]
    tm, place = lax.axis_index("tm"), lax.axis_index("strip")
    moves = [pltpu.make_async_copy(wc_hbm.at[t], wc.at[t], sems.at[t]) for t in range(3)]
    moves.append(pltpu.make_async_copy(wu_hbm, wu, sems.at[3]))
    moves.append(pltpu.make_async_copy(wf_hbm, wf.at[:, pl.ds(0, c1), :], sems.at[4]))
    for move in moves:
        move.start()
    fl, fc = frames + 2, 2 * cols

    gain0 = g0_ref[...]
    blank = jnp.zeros((3, frames + 4, 1, pad_rows, c0), BF)
    acts[:, :, 0:1] = blank
    acts[:, :, cols + 1 :] = blank

    def first(f, _):
        a = prep(x_ref[f].astype(F32).reshape(cols * pad_rows, c0), gain0).astype(F32)
        for k, shift in enumerate((1, 0, cols * pad_rows - 1)):
            moved = pltpu.roll(a, shift, 0) if shift else a
            acts[k, f, pl.ds(1, cols)] = moved.reshape(cols, pad_rows, c0).astype(BF)
        return 0

    lax.fori_loop(0, frames + 4, first, 0)
    wf[:, pl.ds(c1, wf.shape[1] - c1), :] = jnp.zeros((27, wf.shape[1] - c1, c1), BF)
    fblank = jnp.zeros((4, fl, 1, pad_rows, fine.shape[-1]), BF)
    fine[:, :, 0:1] = fblank
    fine[:, :, fc + 1 :] = fblank
    if fine.shape[-1] > c1:
        fine[:, :, :, :, pl.ds(c1, fine.shape[-1] - c1)] = jnp.zeros(
            (4, fl, fc + 2, pad_rows, fine.shape[-1] - c1), BF)

    m = fl * cols * pad_rows
    for t in range(3):
        moves[t].wait()
        for k in range(3):
            lhs = jnp.concatenate(
                [acts[k, t : t + fl, c : c + cols].reshape(m, c0) for c in range(3)], axis=1)
            part = jnp.dot(lhs, wc[t, k].reshape(3 * c0, c0), preferred_element_type=F32)
            if t == 0 and k == 0:
                acc[...] = part + b0_ref[...]
            else:
                acc[...] += part
    row = lax.broadcasted_iota(jnp.int32, (m, 1), 0) % pad_rows + (place * rows - 2)
    keep = (row >= 0) & (row < strips * rows)
    coarse = jnp.where(keep, acc[...], 0.0).astype(BF)

    moves[3].wait()
    for r in range(3):
        for c in range(3):
            prod[r, c] = jnp.dot(coarse, wu[r, c], preferred_element_type=F32).reshape(
                fl, cols, pad_rows, c1)

    frow = 2 * (lax.broadcasted_iota(jnp.int32, (pad_rows, 1), 0) + (place * rows - 2))
    limit = 2 * strips * rows
    bias_u, gain1 = bu_ref[...], g1_ref[...]

    def lift(f, _):
        live = tm * frames + f >= 2
        for col in range(fc):
            j, b = col // 2, col % 2
            q = []
            for r in range(3):
                if b == 0:
                    s = prod[r, 1, f, j] + prod[r, 2, f, j]
                    if j > 0:
                        s = s + prod[r, 0, f, j - 1]
                else:
                    s = prod[r, 0, f, j] + prod[r, 1, f, j]
                    if j < cols - 1:
                        s = s + prod[r, 2, f, j + 1]
                q.append(s)
            pair = (pltpu.roll(q[0], 1, 0) + q[1] + q[2],
                    q[0] + q[1] + pltpu.roll(q[2], pad_rows - 1, 0))
            for a in range(2):
                at = frow + a
                ok = (at >= 0) & (at < limit) & live
                lifted = jnp.where(ok, pair[a] + bias_u, 0.0).astype(BF)
                resid[a, f, col] = lifted
                act = prep(lifted.astype(F32), gain1)
                fine[a, f, col + 1, :, pl.ds(0, c1)] = act
                moved = pltpu.roll(act.astype(F32), pad_rows - 1 if a == 0 else 1, 0)
                fine[3 - a, f, col + 1, :, pl.ds(0, c1)] = moved.astype(BF)
        return 0

    lax.fori_loop(0, fl, lift, 0)

    moves[4].wait()
    kf = fine.shape[-1]
    mf = frames * fc * pad_rows
    for a in range(2):
        planes = (2, 0, 1) if a == 0 else (0, 1, 3)
        for t in range(3):
            for k in range(3):
                lhs = jnp.concatenate(
                    [fine[planes[k], t : t + frames, c : c + fc].reshape(mf, kf) for c in range(3)],
                    axis=1)
                at = (t * 3 + k) * 3
                part = jnp.dot(lhs, wf[at : at + 3].reshape(3 * kf, c1), preferred_element_type=F32)
                if t == 0 and k == 0:
                    facc[...] = part + b1_ref[...]
                else:
                    facc[...] += part
        for f in range(frames):
            size = fc * pad_rows
            total = facc[f * size : (f + 1) * size].reshape(fc, pad_rows, c1)
            total = total + resid[a, f + 2].astype(F32)
            total = jnp.swapaxes(total, 0, 1)[2 : 2 + rows]
            out_ref[f, :, a] = total.astype(BF)


def compute(x, g0, wc, b0, wu, bu, g1, wf, b1, frames, rows, strips):
    cols, pad_rows, c0 = x.shape[1:]
    c1 = wu.shape[-1]
    kf = -(-c1 // 128) * 128
    fl, fc = frames + 2, 2 * cols
    vm = pl.BlockSpec(memory_space=pltpu.VMEM)
    hb = pl.BlockSpec(memory_space=pl.ANY)
    return pl.pallas_call(
        functools.partial(body, (frames, rows, cols, pad_rows, strips)),
        out_shape=jax.ShapeDtypeStruct((frames, rows, 2, fc, c1), BF),
        in_specs=[vm, vm, hb, vm, hb, vm, vm, hb, vm],
        out_specs=vm,
        scratch_shapes=[
            pltpu.VMEM((3, 3, 3, c0, c0), BF),
            pltpu.VMEM((3, 3, c0, c1), BF),
            pltpu.VMEM((27, kf, c1), BF),
            pltpu.VMEM((3, frames + 4, cols + 2, pad_rows, c0), BF),
            pltpu.VMEM((fl * cols * pad_rows, c0), F32),
            pltpu.VMEM((3, 3, fl, cols, pad_rows, c1), F32),
            pltpu.VMEM((4, fl, fc + 2, pad_rows, kf), BF),
            pltpu.VMEM((2, fl, fc, pad_rows, c1), BF),
            pltpu.VMEM((frames * fc * pad_rows, c1), F32),
            pltpu.SemaphoreType.DMA((5,)),
        ],
        compiler_params=pltpu.CompilerParams(vmem_limit_bytes=56 << 20),
    )(x, g0.reshape(1, c0), wc, b0.reshape(1, c0), wu, bu.reshape(1, c1), g1.reshape(1, c1),
      wf.reshape(27, c1, c1), b1.reshape(1, c1))


def local(feat, g0, wc, b0, wu, bu, g1, wf, b1):
    frames, rows, cols, c0 = feat.shape
    c1 = wu.shape[-1]
    tms, strips = lax.axis_size("tm"), lax.axis_size("strip")
    flat = [(i, j) for i in range(tms) for j in range(strips)]

    def send(value, dt, ds):
        pairs = [(i * strips + j, (i + dt) * strips + j + ds) for i, j in flat
                 if 0 <= i + dt < tms and 0 <= j + ds < strips]
        return lax.ppermute(value, ("tm", "strip"), pairs)

    high, low, late = feat[:, :2], feat[:, rows - 2 :], feat[frames - 4 :]
    now = jnp.concatenate([send(low, 0, 1), feat, send(high, 0, -1)], axis=1)
    past = jnp.concatenate([send(low[frames - 4 :], 1, 1), send(late, 1, 0),
                            send(high[frames - 4 :], 1, -1)], axis=1)
    x = jnp.concatenate([past, now], axis=0)
    pad_rows = -(-(rows + 4) // 16) * 16
    x = jnp.pad(x, ((0, 0), (0, pad_rows - rows - 4), (0, 0), (0, 0)))
    x = x.transpose(0, 2, 1, 3)
    out = compute(x, g0, wc, b0, wu, bu, g1, wf, b1, frames, rows, strips)
    return out.reshape(frames, 2 * rows, 2 * cols, c1)


def solution(mesh):
    placed = (P("tm", "strip", None, None), P(), P(), P(), P(), P(), P(), P(), P())
    return jax.shard_map(
        local, mesh=mesh, in_specs=placed, out_specs=P("tm", "strip", None, None), check_vma=False
    )
```

time: 84.2 us -> 40.1 us (0.48)
  the two profiles are of different devices: /device:TPU:9 before, /device:TPU:1 now
where the time goes in v1:
time: 40.1 us; the launch traced here: 39.7 us
  starting transfers between devices  15.8 us (39%)
  Pallas kernels  15.7 us (39%)
  local copies, waits for them, and re-layouts  7.16 us (18%)
  other arithmetic  1 us (2%)
    ppermute x5, starting transfers between devices, send(): return lax.ppermute(value, ('tm', 'strip'), pairs)  15.8 us
    pallas_call x1, Pallas kernels, compute(): pl.pallas_call(functools.partial(body, (frames, rows, cols, pad_rows, str...  15.7 us
    unnamed x2, local copies, waits for them, and re-layouts  4.6 us
    reshape x1, local copies, waits for them, and re-layouts, compute(): b0.reshape(1, c0)  1.27 us
    reshape x1, local copies, waits for them, and re-layouts, compute(): g0.reshape(1, c0)  1.25 us
    transpose x1, other arithmetic, local(): x = x.transpose(0, 2, 1, 3)  1 us
  transfers between devices with their start and end apart: 5, of which 0 were waited for; matrix products, arithmetic and copies ran while one was open for 16% of the time, Pallas kernels for 0%

profile of v1, /device:TPU:1, one launch (start us, length us, event | category | flops | bytes accessed | tf_op | source)
XLA Modules:
  0.0 39.7 jit_solution(1043365510217926568)
XLA Ops:
  0.0 0.9 %copy.10 = bf16[4,12,4,384]{3,1,2,0:T(8,128)(2,1)S(1)} copy(bf16[4,12,4,384]{3,2,1,0:T(4,128)(2,1)} %param.9) | data formatting | bytes 294912 | tf_op args[0]
  0.9 3.9 %collective-permute-start.1 = (bf16[4,12,4,384]{3,1,2,0:T(8,128)(2,1)S(1)}, bf16[4,12,4,384]{3,1,2,0:T(8,128)(2,1)S(1)}, u32[]{:S(2)}, u32[]{:S(2)}) collective-permute-start(bf16[4,12,4,384]{3,1,2,0:T(8,128)(2,1)S(1)} %copy.10), channel_id=1, source_target_pairs={{0,4},{1,5},{2,6},{3,7},{4,8},{5,9},{6,10},{7,11},{8,12},{9,13},{1... | collective-permute-start | bytes 442376 | tf_op jit(solution)/shard_map/ppermute | solution.py:170
  4.9 4.0 %collective-permute-start.3 = (bf16[4,2,4,384]{3,1,2,0:T(2,128)(2,1)S(1)}, bf16[4,2,4,384]{3,1,2,0:T(2,128)(2,1)S(1)}, u32[]{:S(2)}, u32[]{:S(2)}) collective-permute-start(bf16[4,2,4,384]{3,1,2,0:T(2,128)(2,1)S(1)} %get-tuple-element.5), channel_id=1, source_target_pairs={{0,1},{1,2},{2,3},{4,5},{5,6},{6,7},{8,9},{9,10},{10,11},{12,13},{... | collective-permute-start | bytes 73736 | tf_op jit(solution)/shard_map/ppermute | solution.py:170
  8.9 2.9 %collective-permute-start = (bf16[4,2,4,384]{3,1,2,0:T(2,128)(2,1)S(1)}, bf16[4,2,4,384]{3,1,2,0:T(2,128)(2,1)S(1)}, u32[]{:S(2)}, u32[]{:S(2)}) collective-permute-start(bf16[4,2,4,384]{3,1,2,0:T(2,128)(2,1)S(1)} %get-tuple-element.5), channel_id=1, source_target_pairs={{0,5},{1,6},{2,7},{4,9},{5,10},{6,11},{8,13},{9,14},{10,15},{12,17... | collective-permute-start | bytes 73736 | tf_op jit(solution)/shard_map/ppermute | solution.py:170
  11.8 2.6 %collective-permute-start.4 = (bf16[4,2,4,384]{3,1,2,0:T(2,128)(2,1)S(1)}, bf16[4,2,4,384]{3,1,2,0:T(2,128)(2,1)S(1)}, u32[]{:S(2)}, u32[]{:S(2)}) collective-permute-start(bf16[4,2,4,384]{3,1,2,0:T(2,128)(2,1)S(1)} %get-tuple-element.6), channel_id=1, source_target_pairs={{1,0},{2,1},{3,2},{5,4},{6,5},{7,6},{9,8},{10,9},{11,10},{13,12},{... | collective-permute-start | bytes 73736 | tf_op jit(solution)/shard_map/ppermute | solution.py:170
  14.4 2.4 %collective-permute-start.2 = (bf16[4,2,4,384]{3,1,2,0:T(2,128)(2,1)S(1)}, bf16[4,2,4,384]{3,1,2,0:T(2,128)(2,1)S(1)}, u32[]{:S(2)}, u32[]{:S(2)}) collective-permute-start(bf16[4,2,4,384]{3,1,2,0:T(2,128)(2,1)S(1)} %get-tuple-element.6), channel_id=1, source_target_pairs={{1,4},{2,5},{3,6},{5,8},{6,9},{7,10},{9,12},{10,13},{11,14},{13,16... | collective-permute-start | bytes 73736 | tf_op jit(solution)/shard_map/ppermute | solution.py:170
  16.8 1.2 %reshape.21.g0_ref = f32[1,384]{1,0:T(1,128)} reshape(f32[384]{0:T(512)} %param.10) | data formatting | bytes 3072 | tf_op jit(solution)/shard_map/reshape | solution.py:157
  18.1 1.3 %reshape.22.b0_ref = f32[1,384]{1,0:T(1,128)} reshape(f32[384]{0:T(512)} %param.12) | data formatting | bytes 3072 | tf_op jit(solution)/shard_map/reshape | solution.py:157
  19.3 3.7 %copy.14.wu_hbm = bf16[3,3,384,192]{3,2,1,0:T(8,128)(2,1)} copy(bf16[3,3,384,192]{2,3,1,0:T(8,128)(2,1)} %param.13) | data formatting | bytes 2654208 | tf_op args[4]
  23.0 0.0 collective-permute-done.3
  23.0 0.0 collective-permute-done
  23.0 0.0 collective-permute-done.4
  23.0 0.0 collective-permute-done.2
  23.0 0.0 collective-permute-done.1
  23.0 1.0 %maximum_bitcast_fusion.x_ref = bf16[8,4,16,384]{3,2,1,0:T(8,128)(2,1)} fusion(bf16[4,2,4,384]{3,1,2,0:T(2,128)(2,1)S(1)} %collective-permute-done.4, bf16[4,12,4,384]{3,1,2,0:T(8,128)(2,1)S(1)} %copy.10, bf16[4,2,4,384]{3,1,2,0:T(2,128)(2,1)S(1)} %collective-permute-done.3, bf16[4,2,4,384]{3,1,2,0:T(2,128)(2,1)S(1)} %collective-permute-done.2, ...), kind=kLoop, calls=%fused_computation | loop fusion | flops 2359296 | bytes 786432 | tf_op jit(solution)/shard_map/transpose | solution.py:179
  24.0 15.7 %shard_map.91 = bf16[4,12,2,8,192]{4,3,2,1,0:T(8,128)(2,1)} custom-call(bf16[8,4,16,384]{3,2,1,0:T(8,128)(2,1)} %maximum_bitcast_fusion.x_ref, f32[1,384]{1,0:T(1,128)} %reshape.21.g0_ref, bf16[3,3,3,384,384]{4,3,2,1,0:T(8,128)(2,1)} %wc_hbm.1, f32[1,384]{1,0:T(1,128)} %reshape.22.b0_ref, bf16[3,3,384,192]{3,2,1,0:T(8,128)(2,1)} %copy.14.wu_hbm, ...), custom_call_target="tpu_custom_call" | custom-call | tf_op jit(solution)/shard_map/pallas_call | solution.py:139
  (1 shorter events, 0.0 us)
Async XLA Ops:
  0.9 22.1 %collective-permute-start.1 = (bf16[4,12,4,384]{3,1,2,0:T(8,128)(2,1)S(1)}, bf16[4,12,4,384]{3,1,2,0:T(8,128)(2,1)S(1)}, u32[]{:S(2)}, u32[]{:S(2)}) collective-permute-start(bf16[4,12,4,384]{3,1,2,0:T(8,128)(2,1)S(1)} %copy.10), channel_id=1, source_target_pairs={{0,4},{1,5},{2,6},{3,7},{4,8},{5,9},{6,10},{7,11},{8,12},{9,13},{1... | collective-permute-start | bytes 442376 | tf_op jit(solution)/shard_map/ppermute | solution.py:170
  4.9 18.1 %collective-permute-start.3 = (bf16[4,2,4,384]{3,1,2,0:T(2,128)(2,1)S(1)}, bf16[4,2,4,384]{3,1,2,0:T(2,128)(2,1)S(1)}, u32[]{:S(2)}, u32[]{:S(2)}) collective-permute-start(bf16[4,2,4,384]{3,1,2,0:T(2,128)(2,1)S(1)} %get-tuple-element.5), channel_id=1, source_target_pairs={{0,1},{1,2},{2,3},{4,5},{5,6},{6,7},{8,9},{9,10},{10,11},{12,13},{... | collective-permute-start | bytes 73736 | tf_op jit(solution)/shard_map/ppermute | solution.py:170
  8.9 14.1 %collective-permute-start = (bf16[4,2,4,384]{3,1,2,0:T(2,128)(2,1)S(1)}, bf16[4,2,4,384]{3,1,2,0:T(2,128)(2,1)S(1)}, u32[]{:S(2)}, u32[]{:S(2)}) collective-permute-start(bf16[4,2,4,384]{3,1,2,0:T(2,128)(2,1)S(1)} %get-tuple-element.5), channel_id=1, source_target_pairs={{0,5},{1,6},{2,7},{4,9},{5,10},{6,11},{8,13},{9,14},{10,15},{12,17... | collective-permute-start | bytes 73736 | tf_op jit(solution)/shard_map/ppermute | solution.py:170
  11.8 11.2 %collective-permute-start.4 = (bf16[4,2,4,384]{3,1,2,0:T(2,128)(2,1)S(1)}, bf16[4,2,4,384]{3,1,2,0:T(2,128)(2,1)S(1)}, u32[]{:S(2)}, u32[]{:S(2)}) collective-permute-start(bf16[4,2,4,384]{3,1,2,0:T(2,128)(2,1)S(1)} %get-tuple-element.6), channel_id=1, source_target_pairs={{1,0},{2,1},{3,2},{5,4},{6,5},{7,6},{9,8},{10,9},{11,10},{13,12},{... | collective-permute-start | bytes 73736 | tf_op jit(solution)/shard_map/ppermute | solution.py:170
  14.4 8.6 %collective-permute-start.2 = (bf16[4,2,4,384]{3,1,2,0:T(2,128)(2,1)S(1)}, bf16[4,2,4,384]{3,1,2,0:T(2,128)(2,1)S(1)}, u32[]{:S(2)}, u32[]{:S(2)}) collective-permute-start(bf16[4,2,4,384]{3,1,2,0:T(2,128)(2,1)S(1)} %get-tuple-element.6), channel_id=1, source_target_pairs={{1,4},{2,5},{3,6},{5,8},{6,9},{7,10},{9,12},{10,13},{11,14},{13,16... | collective-permute-start | bytes 73736 | tf_op jit(solution)/shard_map/ppermute | solution.py:170

commit v2 on v1

v2 whole, which is shorter than its diff:
```python
import functools

import jax
import jax.numpy as jnp
from jax import lax
from jax.experimental import pallas as pl
from jax.experimental.pallas import tpu as pltpu
from jax.sharding import PartitionSpec as P

eps = 1e-06
F32, BF = jnp.float32, jnp.bfloat16


def prep(values, gain):
    meansq = jnp.mean(values * values, axis=-1, keepdims=True)
    v = values * lax.rsqrt(meansq + eps) * gain
    return (v / (1.0 + jnp.exp(-v))).astype(BF)


def halo(dims, feat, ext, send_sems, recv_sems):
    frames, rows, tms, strips = dims
    tm, place = lax.axis_index("tm"), lax.axis_index("strip")

    def inside(dt, ds):
        return (tm + dt >= 0) & (tm + dt < tms) & (place + ds >= 0) & (place + ds < strips)

    own, late, top, low = (pl.ds(n, k) for n, k in ((4, frames), (frames - 4, 4), (0, 2), (rows - 2, 2)))
    past, every, above, below = pl.ds(0, 4), pl.ds(0, frames), pl.ds(0, 2), pl.ds(rows + 2, 2)
    plan = ((1, 0, (late, pl.ds(0, rows)), (past, pl.ds(2, rows))),
            (0, 1, (every, low), (own, above)),
            (0, -1, (every, top), (own, below)),
            (1, 1, (late, low), (past, above)),
            (1, -1, (late, top), (past, below)))
    barrier = pltpu.get_barrier_semaphore()
    expected = 0
    for dt, ds, _, _ in plan:
        @pl.when(inside(-dt, -ds))
        def _(dt=dt, ds=ds):
            pl.semaphore_signal(barrier, inc=1, device_id=(tm - dt, place - ds),
                                device_id_type=pl.DeviceIdType.MESH)
        expected = expected + inside(dt, ds).astype(jnp.int32)
    pl.semaphore_wait(barrier, expected)

    def move(n):
        dt, ds, src, dst = plan[n]
        return pltpu.make_async_remote_copy(
            src_ref=feat.at[src], dst_ref=ext.at[dst], send_sem=send_sems.at[n],
            recv_sem=recv_sems.at[n], device_id=(tm + dt, place + ds),
            device_id_type=pl.DeviceIdType.MESH)

    for n, (dt, ds, _, _) in enumerate(plan):
        @pl.when(inside(dt, ds))
        def _(n=n):
            move(n).start()

    def finish():
        for n, (dt, ds, _, dst) in enumerate(plan):
            @pl.when(inside(-dt, -ds))
            def _(n=n):
                move(n).wait_recv()

            @pl.when(inside(dt, ds))
            def _(n=n):
                move(n).wait_send()

    def fill():
        ext[own, pl.ds(2, rows)] = feat[...]
        for dt, ds, _, dst in plan:
            @pl.when(jnp.logical_not(inside(-dt, -ds)))
            def _(dst=dst):
                ext[dst] = jnp.zeros((dst[0].size, dst[1].size) + ext.shape[2:], BF)
        spare = ext.shape[1] - rows - 4
        if spare:
            ext[:, pl.ds(rows + 4, spare)] = jnp.zeros((ext.shape[0], spare) + ext.shape[2:], BF)

    return fill, finish


def body(dims, feat_ref, g0_ref, wc_hbm, b0_ref, wu_hbm, bu_ref, g1_ref, wf_hbm, b1_ref, out_ref,
         ext, wc, wu, wf, acts, acc, prod, fine, resid, facc, sems, send_sems, recv_sems):
    frames, rows, cols, pad_rows, tms, strips = dims
    c0, c1 = wc.shape[-1], wf.shape[-1]
    tm, place = lax.axis_index("tm"), lax.axis_index("strip")
    fill, finish = halo((frames, rows, tms, strips), feat_ref, ext, send_sems, recv_sems)
    moves = [pltpu.make_async_copy(wc_hbm.at[t], wc.at[t], sems.at[t]) for t in range(3)]
    moves.append(pltpu.make_async_copy(wu_hbm, wu, sems.at[3]))
    moves.append(pltpu.make_async_copy(wf_hbm, wf.at[:, pl.ds(0, c1), :], sems.at[4]))
    for move in moves:
        move.start()
    fill()
    fl, fc = frames + 2, 2 * cols

    gain0 = g0_ref[...].reshape(1, c0)
    blank = jnp.zeros((3, frames + 4, 1, pad_rows, c0), BF)
    acts[:, :, 0:1] = blank
    acts[:, :, cols + 1 :] = blank

    wf[:, pl.ds(c1, wf.shape[1] - c1), :] = jnp.zeros((27, wf.shape[1] - c1, c1), BF)
    fblank = jnp.zeros((4, fl, 1, pad_rows, fine.shape[-1]), BF)
    fine[:, :, 0:1] = fblank
    fine[:, :, fc + 1 :] = fblank
    if fine.shape[-1] > c1:
        fine[:, :, :, :, pl.ds(c1, fine.shape[-1] - c1)] = jnp.zeros(
            (4, fl, fc + 2, pad_rows, fine.shape[-1] - c1), BF)

    finish()

    def first(f, _):
        x = jnp.swapaxes(ext[f].astype(F32), 0, 1).reshape(cols * pad_rows, c0)
        a = prep(x, gain0).astype(F32)
        for k, shift in enumerate((1, 0, cols * pad_rows - 1)):
            moved = pltpu.roll(a, shift, 0) if shift else a
            acts[k, f, pl.ds(1, cols)] = moved.reshape(cols, pad_rows, c0).astype(BF)
        return 0

    lax.fori_loop(0, frames + 4, first, 0)
    m = fl * cols * pad_rows
    for t in range(3):
        moves[t].wait()
        for k in range(3):
            lhs = jnp.concatenate(
                [acts[k, t : t + fl, c : c + cols].reshape(m, c0) for c in range(3)], axis=1)
            part = jnp.dot(lhs, wc[t, k].reshape(3 * c0, c0), preferred_element_type=F32)
            if t == 0 and k == 0:
                acc[...] = part + b0_ref[...].reshape(1, c0)
            else:
                acc[...] += part
    row = lax.broadcasted_iota(jnp.int32, (m, 1), 0) % pad_rows + (place * rows - 2)
    keep = (row >= 0) & (row < strips * rows)
    coarse = jnp.where(keep, acc[...], 0.0).astype(BF)

    moves[3].wait()
    for r in range(3):
        for c in range(3):
            prod[r, c] = lax.dot_general(
                coarse, wu[r, c], (((1,), (1,)), ((), ())), preferred_element_type=F32).reshape(
                fl, cols, pad_rows, c1)

    frow = 2 * (lax.broadcasted_iota(jnp.int32, (pad_rows, 1), 0) + (place * rows - 2))
    limit = 2 * strips * rows
    bias_u, gain1 = bu_ref[...].reshape(1, c1), g1_ref[...].reshape(1, c1)

    def lift(f, _):
        live = tm * frames + f >= 2
        for col in range(fc):
            j, b = col // 2, col % 2
            q = []
            for r in range(3):
                if b == 0:
                    s = prod[r, 1, f, j] + prod[r, 2, f, j]
                    if j > 0:
                        s = s + prod[r, 0, f, j - 1]
                else:
                    s = prod[r, 0, f, j] + prod[r, 1, f, j]
                    if j < cols - 1:
                        s = s + prod[r, 2, f, j + 1]
                q.append(s)
            pair = (pltpu.roll(q[0], 1, 0) + q[1] + q[2],
                    q[0] + q[1] + pltpu.roll(q[2], pad_rows - 1, 0))
            for a in range(2):
                at = frow + a
                ok = (at >= 0) & (at < limit) & live
                lifted = jnp.where(ok, pair[a] + bias_u, 0.0).astype(BF)
                resid[a, f, col] = lifted
                act = prep(lifted.astype(F32), gain1)
                fine[a, f, col + 1, :, pl.ds(0, c1)] = act
                moved = pltpu.roll(act.astype(F32), pad_rows - 1 if a == 0 else 1, 0)
                fine[3 - a, f, col + 1, :, pl.ds(0, c1)] = moved.astype(BF)
        return 0

    lax.fori_loop(0, fl, lift, 0)

    moves[4].wait()
    kf = fine.shape[-1]
    mf = frames * fc * pad_rows
    for a in range(2):
        planes = (2, 0, 1) if a == 0 else (0, 1, 3)
        for t in range(3):
            for k in range(3):
                lhs = jnp.concatenate(
                    [fine[planes[k], t : t + frames, c : c + fc].reshape(mf, kf) for c in range(3)],
                    axis=1)
                at = (t * 3 + k) * 3
                part = jnp.dot(lhs, wf[at : at + 3].reshape(3 * kf, c1), preferred_element_type=F32)
                if t == 0 and k == 0:
                    facc[...] = part + b1_ref[...].reshape(1, c1)
                else:
                    facc[...] += part
        for f in range(frames):
            size = fc * pad_rows
            total = facc[f * size : (f + 1) * size].reshape(fc, pad_rows, c1)
            total = total + resid[a, f + 2].astype(F32)
            total = jnp.swapaxes(total, 0, 1)[2 : 2 + rows]
            out_ref[f, :, a] = total.astype(BF)


def local(feat, g0, wc, b0, wu, bu, g1, wf, b1):
    frames, rows, cols, c0 = feat.shape
    c1 = wu.shape[-1]
    tms, strips = lax.axis_size("tm"), lax.axis_size("strip")
    pad_rows = -(-(rows + 4) // 16) * 16
    kf = -(-c1 // 128) * 128
    fl, fc = frames + 2, 2 * cols
    vm = pl.BlockSpec(memory_space=pltpu.VMEM)
    hb = pl.BlockSpec(memory_space=pl.ANY)
    out = pl.pallas_call(
        functools.partial(body, (frames, rows, cols, pad_rows, tms, strips)),
        out_shape=jax.ShapeDtypeStruct((frames, rows, 2, fc, c1), BF),
        in_specs=[vm, vm, hb, vm, hb, vm, vm, hb, vm],
        out_specs=vm,
        scratch_shapes=[
            pltpu.VMEM((frames + 4, pad_rows, cols, c0), BF),
            pltpu.VMEM((3, 3, 3, c0, c0), BF),
            pltpu.VMEM((3, 3, c1, c0), BF),
            pltpu.VMEM((27, kf, c1), BF),
            pltpu.VMEM((3, frames + 4, cols + 2, pad_rows, c0), BF),
            pltpu.VMEM((fl * cols * pad_rows, c0), F32),
            pltpu.VMEM((3, 3, fl, cols, pad_rows, c1), F32),
            pltpu.VMEM((4, fl, fc + 2, pad_rows, kf), BF),
            pltpu.VMEM((2, fl, fc, pad_rows, c1), BF),
            pltpu.VMEM((frames * fc * pad_rows, c1), F32),
            pltpu.SemaphoreType.DMA((5,)),
            pltpu.SemaphoreType.DMA((5,)),
            pltpu.SemaphoreType.DMA((5,)),
        ],
        compiler_params=pltpu.CompilerParams(
            vmem_limit_bytes=56 << 20, collective_id=0, has_side_effects=True),
    )(feat, g0, wc, b0, jnp.swapaxes(wu, 2, 3), bu, g1, wf.reshape(27, c1, c1), b1)
    return out.reshape(frames, 2 * rows, fc, c1)


def solution(mesh):
    placed = (P("tm", "strip", None, None), P(), P(), P(), P(), P(), P(), P(), P())
    return jax.shard_map(
        local, mesh=mesh, in_specs=placed, out_specs=P("tm", "strip", None, None), check_vma=False
    )
```

time: 40.1 us -> 26.2 us (0.65)
  the two profiles are of different devices: /device:TPU:1 before, /device:TPU:17 now
where the time goes in v2:
time: 26.2 us; the launch traced here: 26 us
  Pallas kernels  24.2 us (92%)
  local copies, waits for them, and re-layouts  1.77 us (7%)
    pallas_call x1, Pallas kernels, local(): pl.pallas_call(functools.partial(body, (frames, rows, cols, pad_rows, tms...  24.2 us
    unnamed x1, local copies, waits for them, and re-layouts  1.77 us

profile of v2, /device:TPU:17, one launch (start us, length us, event | category | flops | bytes accessed | tf_op | source)
XLA Modules:
  0.0 26.0 jit_solution(6925962099094608917)
XLA Ops:
  0.0 24.2 %shard_map.91 = bf16[4,12,2,8,192]{4,3,2,1,0:T(8,128)(2,1)} custom-call(bf16[4,12,4,384]{3,2,1,0:T(4,128)(2,1)} %feat_ref.1, f32[384]{0:T(512)} %g0_ref.1, bf16[3,3,3,384,384]{4,3,2,1,0:T(8,128)(2,1)} %wc_hbm.1, f32[384]{0:T(512)} %b0_ref.1, bf16[3,3,192,384]{3,2,1,0:T(8,128)(2,1)} %bitcast.5, f32[192]{0:T(256)} %bu_ref.1, f32[192]{0:T(256)} %g1_ref.1, ...), custom_call_target="tpu_custom_call" | custom-call | tf_op jit(solution)/shard_map/pallas_call | solution.py:206
  24.2 1.8 %copy.11 = bf16[4,24,8,192]{3,2,1,0:T(8,128)(2,1)} copy(bf16[4,24,8,192]{3,2,1,0:T(8,128)(2,1)} %bitcast.4) | data formatting | bytes 589824

commit v3 on v2

--- a/solution.py
+++ b/solution.py
@@ -26,11 +26,11 @@
 
     own, late, top, low = (pl.ds(n, k) for n, k in ((4, frames), (frames - 4, 4), (0, 2), (rows - 2, 2)))
     past, every, above, below = pl.ds(0, 4), pl.ds(0, frames), pl.ds(0, 2), pl.ds(rows + 2, 2)
-    plan = ((1, 0, (late, pl.ds(0, rows)), (past, pl.ds(2, rows))),
-            (0, 1, (every, low), (own, above)),
+    plan = ((0, 1, (every, low), (own, above)),
             (0, -1, (every, top), (own, below)),
             (1, 1, (late, low), (past, above)),
-            (1, -1, (late, top), (past, below)))
+            (1, -1, (late, top), (past, below)),
+            (1, 0, (late, pl.ds(0, rows)), (past, pl.ds(2, rows))))
     barrier = pltpu.get_barrier_semaphore()
     expected = 0
     for dt, ds, _, _ in plan:
@@ -53,12 +53,14 @@
         def _(n=n):
             move(n).start()
 
-    def finish():
-        for n, (dt, ds, _, dst) in enumerate(plan):
-            @pl.when(inside(-dt, -ds))
+    def arrive(first, last):
+        for n in range(first, last):
+            @pl.when(inside(-plan[n][0], -plan[n][1]))
             def _(n=n):
                 move(n).wait_recv()
 
+    def depart():
+        for n, (dt, ds, _, _) in enumerate(plan):
             @pl.when(inside(dt, ds))
             def _(n=n):
                 move(n).wait_send()
@@ -73,7 +75,7 @@
         if spare:
             ext[:, pl.ds(rows + 4, spare)] = jnp.zeros((ext.shape[0], spare) + ext.shape[2:], BF)
 
-    return fill, finish
+    return fill, arrive, depart
 
 
 def body(dims, feat_ref, g0_ref, wc_hbm, b0_ref, wu_hbm, bu_ref, g1_ref, wf_hbm, b1_ref, out_ref,
@@ -81,7 +83,7 @@
     frames, rows, cols, pad_rows, tms, strips = dims
     c0, c1 = wc.shape[-1], wf.shape[-1]
     tm, place = lax.axis_index("tm"), lax.axis_index("strip")
-    fill, finish = halo((frames, rows, tms, strips), feat_ref, ext, send_sems, recv_sems)
+    fill, arrive, depart = halo((frames, rows, tms, strips), feat_ref, ext, send_sems, recv_sems)
     moves = [pltpu.make_async_copy(wc_hbm.at[t], wc.at[t], sems.at[t]) for t in range(3)]
     moves.append(pltpu.make_async_copy(wu_hbm, wu, sems.at[3]))
     moves.append(pltpu.make_async_copy(wf_hbm, wf.at[:, pl.ds(0, c1), :], sems.at[4]))
@@ -103,8 +105,6 @@
         fine[:, :, :, :, pl.ds(c1, fine.shape[-1] - c1)] = jnp.zeros(
             (4, fl, fc + 2, pad_rows, fine.shape[-1] - c1), BF)
 
-    finish()
-
     def first(f, _):
         x = jnp.swapaxes(ext[f].astype(F32), 0, 1).reshape(cols * pad_rows, c0)
         a = prep(x, gain0).astype(F32)
@@ -113,28 +113,31 @@
             acts[k, f, pl.ds(1, cols)] = moved.reshape(cols, pad_rows, c0).astype(BF)
         return 0
 
-    lax.fori_loop(0, frames + 4, first, 0)
-    m = fl * cols * pad_rows
-    for t in range(3):
-        moves[t].wait()
-        for k in range(3):
-            lhs = jnp.concatenate(
-                [acts[k, t : t + fl, c : c + cols].reshape(m, c0) for c in range(3)], axis=1)
-            part = jnp.dot(lhs, wc[t, k].reshape(3 * c0, c0), preferred_element_type=F32)
-            if t == 0 and k == 0:
-                acc[...] = part + b0_ref[...].reshape(1, c0)
-            else:
-                acc[...] += part
-    row = lax.broadcasted_iota(jnp.int32, (m, 1), 0) % pad_rows + (place * rows - 2)
-    keep = (row >= 0) & (row < strips * rows)
-    coarse = jnp.where(keep, acc[...], 0.0).astype(BF)
-
-    moves[3].wait()
-    for r in range(3):
-        for c in range(3):
-            prod[r, c] = lax.dot_general(
-                coarse, wu[r, c], (((1,), (1,)), ((), ())), preferred_element_type=F32).reshape(
-                fl, cols, pad_rows, c1)
+    def convolve(lo, hi, fresh):
+        n = hi - lo
+        m = n * cols * pad_rows
+        for t in range(3):
+            if fresh:
+                moves[t].wait()
+            for k in range(3):
+                lhs = jnp.concatenate(
+                    [acts[k, lo + t : hi + t, c : c + cols].reshape(m, c0) for c in range(3)],
+                    axis=1)
+                part = jnp.dot(lhs, wc[t, k].reshape(3 * c0, c0), preferred_element_type=F32)
+                if t == 0 and k == 0:
+                    acc[:m] = part + b0_ref[...].reshape(1, c0)
+                else:
+                    acc[:m] += part
+        row = lax.broadcasted_iota(jnp.int32, (m, 1), 0) % pad_rows + (place * rows - 2)
+        keep = (row >= 0) & (row < strips * rows)
+        coarse = jnp.where(keep, acc[:m], 0.0).astype(BF)
+        if fresh:
+            moves[3].wait()
+        for r in range(3):
+            for c in range(3):
+                prod[r, c, lo:hi] = lax.dot_general(
+                    coarse, wu[r, c], (((1,), (1,)), ((), ())), preferred_element_type=F32
+                ).reshape(n, cols, pad_rows, c1)
 
     frow = 2 * (lax.broadcasted_iota(jnp.int32, (pad_rows, 1), 0) + (place * rows - 2))
     limit = 2 * strips * rows
@@ -168,7 +171,14 @@
                 fine[3 - a, f, col + 1, :, pl.ds(0, c1)] = moved.astype(BF)
         return 0
 
-    lax.fori_loop(0, fl, lift, 0)
+    arrive(0, 2)
+    lax.fori_loop(4, frames + 4, first, 0)
+    convolve(4, fl, True)
+    lax.fori_loop(4, fl, lift, 0)
+    arrive(2, 5)
+    lax.fori_loop(0, 4, first, 0)
+    convolve(0, 4, False)
+    lax.fori_loop(0, 4, lift, 0)
 
     moves[4].wait()
     kf = fine.shape[-1]
@@ -192,6 +202,7 @@
             total = total + resid[a, f + 2].astype(F32)
             total = jnp.swapaxes(total, 0, 1)[2 : 2 + rows]
             out_ref[f, :, a] = total.astype(BF)
+    depart()
 
 
 def local(feat, g0, wc, b0, wu, bu, g1, wf, b1):

time: 26.2 us -> 23.2 us (0.89)
  the two profiles are of different devices: /device:TPU:17 before, /device:TPU:1 now
where the time goes in v3:
time: 23.2 us; the launch traced here: 23.1 us
  Pallas kernels  21.3 us (92%)
  local copies, waits for them, and re-layouts  1.77 us (8%)
    pallas_call x1, Pallas kernels, local(): pl.pallas_call(functools.partial(body, (frames, rows, cols, pad_rows, tms...  21.3 us
    unnamed x1, local copies, waits for them, and re-layouts  1.77 us

profile of v3, /device:TPU:1, one launch (start us, length us, event | category | flops | bytes accessed | tf_op | source)
XLA Modules:
  0.0 23.1 jit_solution(10736812078589903371)
XLA Ops:
  0.0 21.3 %shard_map.91 = bf16[4,12,2,8,192]{4,3,2,1,0:T(8,128)(2,1)} custom-call(bf16[4,12,4,384]{3,2,1,0:T(4,128)(2,1)} %feat_ref.1, f32[384]{0:T(512)} %g0_ref.1, bf16[3,3,3,384,384]{4,3,2,1,0:T(8,128)(2,1)} %wc_hbm.1, f32[384]{0:T(512)} %b0_ref.1, bf16[3,3,192,384]{3,2,1,0:T(8,128)(2,1)} %bitcast.5, f32[192]{0:T(256)} %bu_ref.1, f32[192]{0:T(256)} %g1_ref.1, ...), custom_call_target="tpu_custom_call" | custom-call | tf_op jit(solution)/shard_map/pallas_call | solution.py:217
  21.3 1.8 %copy.11 = bf16[4,24,8,192]{3,2,1,0:T(8,128)(2,1)} copy(bf16[4,24,8,192]{3,2,1,0:T(8,128)(2,1)} %bitcast.4) | data formatting | bytes 589824

commit v4 on v3

--- a/solution.py
+++ b/solution.py
@@ -66,7 +66,6 @@
                 move(n).wait_send()
 
     def fill():
-        ext[own, pl.ds(2, rows)] = feat[...]
         for dt, ds, _, dst in plan:
             @pl.when(jnp.logical_not(inside(-dt, -ds)))
             def _(dst=dst):
@@ -78,21 +77,24 @@
     return fill, arrive, depart
 
 
-def body(dims, feat_ref, g0_ref, wc_hbm, b0_ref, wu_hbm, bu_ref, g1_ref, wf_hbm, b1_ref, out_ref,
-         ext, wc, wu, wf, acts, acc, prod, fine, resid, facc, sems, send_sems, recv_sems):
+def body(dims, feat_ref, g0_hbm, wc_hbm, b0_hbm, wu_hbm, bu_hbm, g1_hbm, wf_hbm, b1_hbm, out_ref,
+         ext, g0_ref, b0_ref, bu_ref, g1_ref, b1_ref, wc, wu, wf, acts, acc, prod, fine, resid, facc, sems, send_sems, recv_sems):
     frames, rows, cols, pad_rows, tms, strips = dims
     c0, c1 = wc.shape[-1], wf.shape[-1]
     tm, place = lax.axis_index("tm"), lax.axis_index("strip")
     fill, arrive, depart = halo((frames, rows, tms, strips), feat_ref, ext, send_sems, recv_sems)
+    own = ext.at[pl.ds(4, frames), pl.ds(2, rows)]
+    small = [pltpu.make_async_copy(src, dst, sems.at[5 + n]) for n, (src, dst) in enumerate((
+        (feat_ref, own), (g0_hbm, g0_ref), (b0_hbm, b0_ref), (bu_hbm, bu_ref), (g1_hbm, g1_ref),
+        (b1_hbm, b1_ref)))]
     moves = [pltpu.make_async_copy(wc_hbm.at[t], wc.at[t], sems.at[t]) for t in range(3)]
     moves.append(pltpu.make_async_copy(wu_hbm, wu, sems.at[3]))
     moves.append(pltpu.make_async_copy(wf_hbm, wf.at[:, pl.ds(0, c1), :], sems.at[4]))
-    for move in moves:
+    for move in small + moves:
         move.start()
     fill()
     fl, fc = frames + 2, 2 * cols
 
-    gain0 = g0_ref[...].reshape(1, c0)
     blank = jnp.zeros((3, frames + 4, 1, pad_rows, c0), BF)
     acts[:, :, 0:1] = blank
     acts[:, :, cols + 1 :] = blank
@@ -107,7 +109,7 @@
 
     def first(f, _):
         x = jnp.swapaxes(ext[f].astype(F32), 0, 1).reshape(cols * pad_rows, c0)
-        a = prep(x, gain0).astype(F32)
+        a = prep(x, g0_ref[...].reshape(1, c0)).astype(F32)
         for k, shift in enumerate((1, 0, cols * pad_rows - 1)):
             moved = pltpu.roll(a, shift, 0) if shift else a
             acts[k, f, pl.ds(1, cols)] = moved.reshape(cols, pad_rows, c0).astype(BF)
@@ -141,7 +143,6 @@
 
     frow = 2 * (lax.broadcasted_iota(jnp.int32, (pad_rows, 1), 0) + (place * rows - 2))
     limit = 2 * strips * rows
-    bias_u, gain1 = bu_ref[...].reshape(1, c1), g1_ref[...].reshape(1, c1)
 
     def lift(f, _):
         live = tm * frames + f >= 2
@@ -163,14 +164,16 @@
             for a in range(2):
                 at = frow + a
                 ok = (at >= 0) & (at < limit) & live
-                lifted = jnp.where(ok, pair[a] + bias_u, 0.0).astype(BF)
+                lifted = jnp.where(ok, pair[a] + bu_ref[...].reshape(1, c1), 0.0).astype(BF)
                 resid[a, f, col] = lifted
-                act = prep(lifted.astype(F32), gain1)
+                act = prep(lifted.astype(F32), g1_ref[...].reshape(1, c1))
                 fine[a, f, col + 1, :, pl.ds(0, c1)] = act
                 moved = pltpu.roll(act.astype(F32), pad_rows - 1 if a == 0 else 1, 0)
                 fine[3 - a, f, col + 1, :, pl.ds(0, c1)] = moved.astype(BF)
         return 0
 
+    for move in small:
+        move.wait()
     arrive(0, 2)
     lax.fori_loop(4, frames + 4, first, 0)
     convolve(4, fl, True)
@@ -213,14 +216,19 @@
     kf = -(-c1 // 128) * 128
     fl, fc = frames + 2, 2 * cols
     vm = pl.BlockSpec(memory_space=pltpu.VMEM)
-    hb = pl.BlockSpec(memory_space=pl.ANY)
+    hb = pl.BlockSpec(memory_space=pltpu.HBM)
     out = pl.pallas_call(
         functools.partial(body, (frames, rows, cols, pad_rows, tms, strips)),
         out_shape=jax.ShapeDtypeStruct((frames, rows, 2, fc, c1), BF),
-        in_specs=[vm, vm, hb, vm, hb, vm, vm, hb, vm],
+        in_specs=[hb] * 9,
         out_specs=vm,
         scratch_shapes=[
             pltpu.VMEM((frames + 4, pad_rows, cols, c0), BF),
+            pltpu.VMEM((c0,), F32),
+            pltpu.VMEM((c0,), F32),
+            pltpu.VMEM((c1,), F32),
+            pltpu.VMEM((c1,), F32),
+            pltpu.VMEM((c1,), F32),
             pltpu.VMEM((3, 3, 3, c0, c0), BF),
             pltpu.VMEM((3, 3, c1, c0), BF),
             pltpu.VMEM((27, kf, c1), BF),
@@ -230,7 +238,7 @@
             pltpu.VMEM((4, fl, fc + 2, pad_rows, kf), BF),
             pltpu.VMEM((2, fl, fc, pad_rows, c1), BF),
             pltpu.VMEM((frames * fc * pad_rows, c1), F32),
-            pltpu.SemaphoreType.DMA((5,)),
+            pltpu.SemaphoreType.DMA((11,)),
             pltpu.SemaphoreType.DMA((5,)),
             pltpu.SemaphoreType.DMA((5,)),
         ],

time: 23.2 us -> 22.6 us (0.974)
  Pallas kernels: 21.3 us -> 20.7 us
    pallas_call x1, Pallas kernels: 21.3 us -> 20.7 us  [local(): pl.pallas_call(functools.partial(body, (frames, rows, cols, pad_rows, tms...]
where the time goes in v4:
time: 22.6 us; the launch traced here: 22.4 us
  Pallas kernels  20.7 us (92%)
  local copies, waits for them, and re-layouts  1.77 us (8%)
    pallas_call x1, Pallas kernels, local(): pl.pallas_call(functools.partial(body, (frames, rows, cols, pad_rows, tms...  20.7 us
    unnamed x1, local copies, waits for them, and re-layouts  1.77 us

profile of v4, /device:TPU:1, one launch (start us, length us, event | category | flops | bytes accessed | tf_op | source)
XLA Modules:
  0.0 22.4 jit_solution(14182514591377440237)
XLA Ops:
  0.0 20.7 %shard_map.91 = bf16[4,12,2,8,192]{4,3,2,1,0:T(8,128)(2,1)} custom-call(bf16[4,12,4,384]{3,2,1,0:T(4,128)(2,1)} %feat_ref.1, f32[384]{0:T(512)} %g0_hbm.1, bf16[3,3,3,384,384]{4,3,2,1,0:T(8,128)(2,1)} %wc_hbm.1, f32[384]{0:T(512)} %b0_hbm.1, bf16[3,3,192,384]{3,2,1,0:T(8,128)(2,1)} %bitcast.5, f32[192]{0:T(256)} %bu_hbm.1, f32[192]{0:T(256)} %g1_hbm.1, ...), custom_call_target="tpu_custom_call" | custom-call | tf_op jit(solution)/shard_map/pallas_call | solution.py:220
  20.7 1.8 %copy.11 = bf16[4,24,8,192]{3,2,1,0:T(8,128)(2,1)} copy(bf16[4,24,8,192]{3,2,1,0:T(8,128)(2,1)} %bitcast.4) | data formatting | bytes 589824
